TPU v7x, 256 devices: a whole 4x4x8 slice. The times are simulated.
256 devices in a mesh: gx: 8 (over z_lo, y), gy: 8 (over x, core), dir: 4 (over z_hi).
Axes of the slice: x: 4, y: 4, z: 8 (z_hi: 4, z_lo: 2; z = z_hi * 2 + z_lo), core: 2. Of those that a mesh axis runs over, the one named last changes fastest.
Arguments:
- directions: float32 [32, 1024, 2048], P('dir', 'gx', 'gy'), may hold values from -6 to 6
- velocity: float32 [2, 1024, 2048], P(None, 'gx', 'gy'), may hold values from -6 to 6
- viscosity: float32 [1024, 2048], P('gx', 'gy'), may hold values from 0.5 to 2
- basal_drag: float32 [1024, 2048], P('gx', 'gy'), may hold values from 0.5 to 8
- misfit_weight: float32 [1024, 2048], P('gx', 'gy'), may hold values from 1 to 10
- ice_mask: int32 [1024, 2048], P('gx', 'gy'), may hold values 0 or 1
- grounded: int32 [1024, 2048], P('gx', 'gy'), may hold values 0 or 1
Outputs:
- basis: float32 [32, 1024, 2048], P('dir', 'gx', 'gy')
- upper: float32 [32, 32], replicated
All inputs are finite; a program needn't handle non-finite values. No bound on the sum of `ice_mask` or of `grounded` on one device may be relied on, other than what follows from the above.
Results may differ from a plain program's by a relative error of at most 0.00021.
Values sent between devices are 32-bit elements; how exact they have to be, the bound alone decides.
A program may use at most 64 MiB of HBM per device.

v0:
```python
import jax
import jax.numpy as jnp
from jax import lax
from jax.sharding import PartitionSpec as P

SWEEPS = 6
damping = 0.8


def with_halo(value, sides, width):
    for axis, dim in sides:
        count, length = (lax.axis_size(axis), value.shape[dim])
        up = [(i, (i + 1) % count) for i in range(count - 1)]
        down = [(j, i) for i, j in up]
        last = lax.slice_in_dim(value, length - width, length, axis=dim)
        first = lax.slice_in_dim(value, 0, width, axis=dim)
        before = lax.ppermute(last, axis, up)
        after = lax.ppermute(first, axis, down)
        value = jnp.concatenate([before, value, after], axis=dim)
    return value


def weights_pair():
    along_x = jnp.array([4.0, 1.0], jnp.float32).reshape(2, 1, 1)
    along_y = jnp.array([1.0, 4.0], jnp.float32).reshape(2, 1, 1)
    return (along_x, along_y)


def relax_sweep(state, padded, coeffs, source):
    face_east, face_west, face_north, face_south, friction, diagonal, ice_keep = coeffs
    along_x, along_y = weights_pair()
    next_row = padded[..., 2:, 1:-1]
    prev_row = padded[..., :-2, 1:-1]
    next_col = padded[..., 1:-1, 2:]
    prev_col = padded[..., 1:-1, :-2]
    applied = along_x * (face_east * (state - next_row) + face_west * (state - prev_row))
    applied = applied + along_y * (
        face_north * (state - next_col) + face_south * (state - prev_col)
    )
    applied = applied + friction * state
    return ice_keep * (state + damping * (source - applied) / diagonal)


def solve_shared(source, coeffs):
    diagonal, ice_keep = (coeffs[5], coeffs[6])
    state = ice_keep * damping * source / diagonal
    for sweep in range(SWEEPS - 1):
        padded = with_halo(state, (("gx", 2), ("gy", 3)), 1)
        state = relax_sweep(state, padded, coeffs, source)
    return state


def make_coeffs(viscosity, padded_visc, basal_drag, grounded_f):
    face_east = 0.5 * (viscosity + padded_visc[2:, 1:-1])
    face_west = 0.5 * (viscosity + padded_visc[:-2, 1:-1])
    face_north = 0.5 * (viscosity + padded_visc[1:-1, 2:])
    face_south = 0.5 * (viscosity + padded_visc[1:-1, :-2])
    friction = basal_drag * grounded_f
    along_x, along_y = weights_pair()
    diagonal = along_x * (face_east + face_west) + along_y * (face_north + face_south) + friction
    return (face_east, face_west, face_north, face_south, friction, diagonal)


def on_device(directions, velocity, viscosity, basal_drag, misfit_weight, ice_mask, grounded):
    own_count = directions.shape[0]
    tile_rows = directions.shape[1]
    tile_cols = directions.shape[2]
    padded_visc = with_halo(viscosity, (("gx", 0), ("gy", 1)), 1)
    ice_keep = ice_mask.astype(jnp.float32)
    face_east, face_west, face_north, face_south, friction, diagonal = make_coeffs(
        viscosity, padded_visc, basal_drag, grounded.astype(jnp.float32)
    )
    coeffs = (face_east, face_west, face_north, face_south, friction, diagonal, ice_keep)
    forward = solve_shared(-friction * velocity[None] * directions[:, None], coeffs)
    adjoint = solve_shared(misfit_weight * forward, coeffs)
    sketch = -friction * jnp.sum(velocity[None] * adjoint, axis=1)
    cells = tile_rows * tile_cols
    total_cells = cells * lax.axis_size("gx") * lax.axis_size("gy")
    own_flat = sketch.reshape(own_count, cells)
    identity = jnp.eye(own_count * lax.axis_size("dir"), dtype=jnp.float32)
    whole = lax.all_gather(own_flat, "dir", axis=0, tiled=True)
    gram_local = jnp.dot(
        whole, whole.T, precision=lax.Precision.HIGHEST, preferred_element_type=jnp.float32
    )
    gram_sum = lax.psum(gram_local, ("gx", "gy"))
    lower = jnp.linalg.cholesky(gram_sum / jnp.float32(total_cells))
    inverse = lax.linalg.triangular_solve(lower, identity, left_side=True, lower=True)
    own_rows = lax.dynamic_slice_in_dim(inverse, lax.axis_index("dir") * own_count, own_count, 0)
    basis_flat = jnp.dot(
        own_rows, whole, precision=lax.Precision.HIGHEST, preferred_element_type=jnp.float32
    )
    return (basis_flat.reshape(own_count, tile_rows, tile_cols), lower.T)


def solution(mesh):
    placed = (
        P("dir", "gx", "gy"),
        P(None, "gx", "gy"),
        P("gx", "gy"),
        P("gx", "gy"),
        P("gx", "gy"),
        P("gx", "gy"),
        P("gx", "gy"),
    )
    return jax.shard_map(
        on_device,
        mesh=mesh,
        in_specs=placed,
        out_specs=(P("dir", "gx", "gy"), P()),
        check_vma=False,
    )
```

profile of v0, /device:TPU:64, one launch (start us, length us, event | category | flops | bytes accessed | tf_op | source)
XLA Modules:
  0.0 741.2 jit_solution(18365183644680429997)
XLA Ops:
  9.3 4.5 collective-permute-start.1
  17.9 3.0 collective-permute-start.3
  25.3 4.5 collective-permute-start.5
  33.4 1.9 copy.100
  37.2 3.0 collective-permute-start.7
  44.3 7.2 fusion.4
  52.8 5.0 collective-permute-start.9
  61.5 2.5 copy.104
  65.2 2.5 copy.106
  67.7 4.8 collective-permute-start.11
  72.6 2.4 copy.105
  74.9 2.3 copy.107
  77.2 5.3 fusion.8
  83.9 4.8 collective-permute-start.13
  92.3 2.6 copy.108
  96.3 2.5 copy.110
  98.7 4.1 collective-permute-start.15
  102.9 2.4 copy.109
  105.3 2.4 copy.111
  107.6 5.3 fusion.12
  114.2 6.7 collective-permute-start.17
  124.6 2.6 copy.112
  128.5 2.5 copy.114
  131.0 3.6 collective-permute-start.19
  134.6 2.4 copy.113
  137.0 2.4 copy.115
  139.4 5.3 fusion.16
  146.0 6.9 collective-permute-start.21
  156.5 1.9 copy.116
  160.3 3.0 collective-permute-start.23
  166.7 8.1 %multiply_divide_fusion = (f32[8,2,128,256]{3,0,2,1:T(8,128)S(1)}, f32[8,2,128,256]{3,0,2,1:T(8,128)S(1)}) fusion(f32[2,128,256]{2,1,0:T(8,128)S(1)} %get-tuple-element.69, f32[128,256]{1,0:T(8,128)} %copy-done.17, f32[8,2,128,256]{3,0,2,1:T(8,128)} %copy-done.9, f32[128,256]{1,0:T(8,128)S(1)} %get-tuple-element.11, ...), kind=kLoop, calls=%fused_computation.279 | loop fusion | flops 16777216 | bytes 8962320 | tf_op jit(solution)/shard_map/div | solution.py:46
  176.1 6.7 collective-permute-start.25
  186.2 1.9 copy.120
  189.4 1.9 copy.122
  191.3 3.6 collective-permute-start.27
  198.2 7.3 fusion.182
  206.9 6.9 collective-permute-start.29
  217.1 1.9 copy.124
  220.3 1.9 copy.126
  222.2 4.0 collective-permute-start.31
  229.5 7.0 fusion.183
  237.8 6.7 collective-permute-start.33
  247.8 1.9 copy.128
  251.0 1.9 copy.130
  252.8 3.8 collective-permute-start.35
  260.0 7.0 fusion.184
  268.3 6.9 collective-permute-start.37
  278.5 1.9 copy.132
  281.9 1.9 copy.134
  283.8 4.0 collective-permute-start.39
  291.2 7.0 fusion.185
  299.5 6.9 collective-permute-start.41
  310.1 2.5 copy.136
  313.9 2.5 copy.138
  316.4 4.6 collective-permute-start.43
  322.0 2.4 copy.137
  324.3 2.4 copy.139
  326.7 7.1 multiply_reduce_fusion
  335.0 99.5 %all-gather.2.cloned.1.call-done = f32[32,32768]{1,0:T(8,128)} async-done(((f32[8,32768]{1,0:T(8,128)}), f32[32,32768]{1,0:T(8,128)}) %all-gather.2.cloned.1.call-update) | async-done | bytes 4194320 | tf_op jit(solution)/shard_map/all_gather | solution.py:81
  434.4 6.9 fusion.230
  441.4 279.7 %psum.7 = f32[32,32]{0,1:T(8,128)S(1)} all-reduce(f32[32,32]{0,1:T(8,128)S(1)} %fusion.230), channel_id=1, replica_groups=mesh['gx'=8,'gy'=8,'dir'=4] {'gx','gy'}, use_global_device_ids=true, to_apply=%region_1.0 | all-reduce | flops 1024 | bytes 8192 | tf_op jit(solution)/shard_map/psum | solution.py:85
  721.2 2.9 cholesky.17
  725.4 2.4 custom-call.6
  728.1 3.8 fusion.198
  (200 shorter events, 97.6 us)
Async XLA Ops:
  7.2 15.4 %copy-start.21 = (f32[128,256]{1,0:T(8,128)S(1)}, f32[128,256]{1,0:T(8,128)}, u32[]{:S(2)}) copy-start(f32[128,256]{1,0:T(8,128)} %param.31) | copy-start | bytes 393220
  7.2 14.7 %copy-start.18 = (f32[8,128,256]{2,1,0:T(8,128)S(1)}, f32[8,128,256]{2,1,0:T(8,128)}, u32[]{:S(2)}) copy-start(f32[8,128,256]{2,1,0:T(8,128)} %param.29) | copy-start | bytes 3145732
  7.2 427.3 %all-gather.2.cloned.1.call-start = ((), (), s32[]{:S(2)}) async-start(), calls=%async_computation | async-start | bytes 5242880 | tf_op jit(solution)/shard_map/all_gather | solution.py:81
  8.0 7.5 %collective-permute-start = (f32[1,256]{1,0:T(1,128)S(1)}, f32[1,256]{1,0:T(1,128)S(1)}, u32[]{:S(2)}, u32[]{:S(2)}) collective-permute-start(f32[1,256]{1,0:T(1,128)S(1)} %get-tuple-element.66), channel_id=1, source_target_pairs={{32,0},{64,32},{96,64},{128,96},{160,128},{192,160},{224,192},{33,... | collective-permute-start | bytes 3080 | tf_op jit(solution)/shard_map/ppermute | solution.py:18
  9.3 6.2 collective-permute-start.1
  16.6 5.9 collective-permute-start.2
  17.9 4.6 collective-permute-start.3
  24.0 5.9 collective-permute-start.4
  25.3 6.0 collective-permute-start.5
  35.3 5.7 collective-permute-start.6
  37.2 5.4 collective-permute-start.7
  51.5 6.3 collective-permute-start.8
  52.8 6.4 collective-permute-start.9
  64.0 8.6 %collective-permute-start.10 = (f32[8,2,130,1]{2,0,3,1:T(8,128)}, f32[8,2,130,1]{2,0,3,1:T(8,128)}, u32[]{:S(2)}, u32[]{:S(2)}) collective-permute-start(f32[8,2,130,1]{2,0,3,1:T(8,128)} %copy.104), channel_id=1, source_target_pairs={{4,0},{8,4},{12,8},{16,12},{20,16},{24,20},{28,24},{5,1},{9,5},{13... | collective-permute-start | bytes 24968 | tf_op jit(solution)/shard_map/ppermute | solution.py:18
  67.7 7.2 collective-permute-start.11
  82.6 6.1 collective-permute-start.12
  83.9 6.2 collective-permute-start.13
  92.3 15.3 %copy-start.2 = (f32[8,2,128,256]{3,0,2,1:T(8,128)S(1)}, f32[8,2,128,256]{3,0,2,1:T(8,128)}, u32[]{:S(2)}) copy-start(f32[8,2,128,256]{3,0,2,1:T(8,128)} %copy-done.1) | copy-start | bytes 6291460
  95.0 7.9 %collective-permute-start.14 = (f32[8,2,130,1]{2,0,3,1:T(8,128)}, f32[8,2,130,1]{2,0,3,1:T(8,128)}, u32[]{:S(2)}, u32[]{:S(2)}) collective-permute-start(f32[8,2,130,1]{2,0,3,1:T(8,128)} %copy.108), channel_id=1, source_target_pairs={{4,0},{8,4},{12,8},{16,12},{20,16},{24,20},{28,24},{5,1},{9,5},{13... | collective-permute-start | bytes 24968 | tf_op jit(solution)/shard_map/ppermute | solution.py:18
  98.7 6.5 collective-permute-start.15
  112.9 9.6 %copy-start.3 = (f32[8,2,128,256]{3,0,2,1:T(8,128)}, f32[8,2,128,256]{3,0,2,1:T(8,128)S(1)}, u32[]{:S(2)}) copy-start(f32[8,2,128,256]{3,0,2,1:T(8,128)S(1)} %fusion.12) | copy-start | bytes 6291460
  112.9 8.0 %collective-permute-start.16 = (f32[8,2,1,256]{3,0,2,1:T(8,128)S(1)}, f32[8,2,1,256]{3,0,2,1:T(8,128)S(1)}, u32[]{:S(2)}, u32[]{:S(2)}) collective-permute-start(f32[8,2,1,256]{3,0,2,1:T(8,128)S(1)} %get-tuple-element.53), channel_id=1, source_target_pairs={{32,0},{64,32},{96,64},{128,96},{160,128},{192,160},{224,192},{33,... | collective-permute-start | bytes 49160 | tf_op jit(solution)/shard_map/ppermute | solution.py:18
  114.2 8.1 %collective-permute-start.17 = (f32[8,2,1,256]{3,0,2,1:T(8,128)S(1)}, f32[8,2,1,256]{3,0,2,1:T(8,128)S(1)}, u32[]{:S(2)}, u32[]{:S(2)}) collective-permute-start(f32[8,2,1,256]{3,0,2,1:T(8,128)S(1)} %get-tuple-element.52), channel_id=1, source_target_pairs={{0,32},{32,64},{64,96},{96,128},{128,160},{160,192},{192,224},{1,3... | collective-permute-start | bytes 49160 | tf_op jit(solution)/shard_map/ppermute | solution.py:17
  124.6 14.8 %copy-start.4 = (f32[8,2,128,256]{3,0,2,1:T(8,128)S(1)}, f32[8,2,128,256]{3,0,2,1:T(8,128)}, u32[]{:S(2)}) copy-start(f32[8,2,128,256]{3,0,2,1:T(8,128)} %copy-done.3) | copy-start | bytes 6291460
  127.2 7.4 collective-permute-start.18
  131.0 6.0 collective-permute-start.19
  144.7 10.4 %copy-start.9 = (f32[8,2,128,256]{3,0,2,1:T(8,128)}, f32[8,2,128,256]{3,0,2,1:T(8,128)S(1)}, u32[]{:S(2)}) copy-start(f32[8,2,128,256]{3,0,2,1:T(8,128)S(1)} %fusion.16) | copy-start | bytes 6291460
  144.7 8.2 %collective-permute-start.20 = (f32[8,2,1,256]{3,0,2,1:T(8,128)S(1)}, f32[8,2,1,256]{3,0,2,1:T(8,128)S(1)}, u32[]{:S(2)}, u32[]{:S(2)}) collective-permute-start(f32[8,2,1,256]{3,0,2,1:T(8,128)S(1)} %get-tuple-element.51), channel_id=1, source_target_pairs={{32,0},{64,32},{96,64},{128,96},{160,128},{192,160},{224,192},{33,... | collective-permute-start | bytes 49160 | tf_op jit(solution)/shard_map/ppermute | solution.py:18
  146.0 8.4 %collective-permute-start.21 = (f32[8,2,1,256]{3,0,2,1:T(8,128)S(1)}, f32[8,2,1,256]{3,0,2,1:T(8,128)S(1)}, u32[]{:S(2)}, u32[]{:S(2)}) collective-permute-start(f32[8,2,1,256]{3,0,2,1:T(8,128)S(1)} %get-tuple-element.50), channel_id=1, source_target_pairs={{0,32},{32,64},{64,96},{96,128},{128,160},{160,192},{192,224},{1,3... | collective-permute-start | bytes 49160 | tf_op jit(solution)/shard_map/ppermute | solution.py:17
  158.3 5.0 collective-permute-start.22
  160.3 4.7 collective-permute-start.23
  174.8 9.6 %copy-start.10 = (f32[8,2,128,256]{3,0,2,1:T(8,128)}, f32[8,2,128,256]{3,0,2,1:T(8,128)S(1)}, u32[]{:S(2)}) copy-start(f32[8,2,128,256]{3,0,2,1:T(8,128)S(1)} %get-tuple-element.12) | copy-start | bytes 6291460
  174.8 8.0 %collective-permute-start.24 = (f32[8,2,1,256]{3,0,2,1:T(8,128)S(1)}, f32[8,2,1,256]{3,0,2,1:T(8,128)S(1)}, u32[]{:S(2)}, u32[]{:S(2)}) collective-permute-start(f32[8,2,1,256]{3,0,2,1:T(8,128)S(1)} %get-tuple-element.49), channel_id=1, source_target_pairs={{32,0},{64,32},{96,64},{128,96},{160,128},{192,160},{224,192},{33,... | collective-permute-start | bytes 49160 | tf_op jit(solution)/shard_map/ppermute | solution.py:18
  176.1 8.1 %collective-permute-start.25 = (f32[8,2,1,256]{3,0,2,1:T(8,128)S(1)}, f32[8,2,1,256]{3,0,2,1:T(8,128)S(1)}, u32[]{:S(2)}, u32[]{:S(2)}) collective-permute-start(f32[8,2,1,256]{3,0,2,1:T(8,128)S(1)} %get-tuple-element.48), channel_id=1, source_target_pairs={{0,32},{32,64},{64,96},{96,128},{128,160},{160,192},{192,224},{1,3... | collective-permute-start | bytes 49160 | tf_op jit(solution)/shard_map/ppermute | solution.py:17
  186.1 12.1 %copy-start.11 = (f32[128,256]{1,0:T(8,128)S(1)}, f32[128,256]{1,0:T(8,128)}, u32[]{:S(2)}) copy-start(f32[128,256]{1,0:T(8,128)} %convert_element_type.8) | copy-start | bytes 393220
  186.1 12.1 %copy-start.12 = (f32[128,256]{1,0:T(8,128)S(1)}, f32[128,256]{1,0:T(8,128)}, u32[]{:S(2)}) copy-start(f32[128,256]{1,0:T(8,128)} %get-tuple-element.15) | copy-start | bytes 393220
  186.1 12.1 %copy-start.13 = (f32[128,256]{1,0:T(8,128)S(1)}, f32[128,256]{1,0:T(8,128)}, u32[]{:S(2)}) copy-start(f32[128,256]{1,0:T(8,128)} %get-tuple-element.16) | copy-start | bytes 393220
  186.1 12.1 %copy-start.14 = (f32[128,256]{1,0:T(8,128)S(1)}, f32[128,256]{1,0:T(8,128)}, u32[]{:S(2)}) copy-start(f32[128,256]{1,0:T(8,128)} %get-tuple-element.63) | copy-start | bytes 393220
  186.1 12.1 %copy-start.15 = (f32[128,256]{1,0:T(8,128)S(1)}, f32[128,256]{1,0:T(8,128)}, u32[]{:S(2)}) copy-start(f32[128,256]{1,0:T(8,128)} %get-tuple-element.64) | copy-start | bytes 393220
  186.1 12.1 %copy-start.30 = (f32[2]{0:T(128)S(1)}, f32[2]{0:T(128)}, u32[]{:S(2)}) copy-start(f32[2]{0:T(128)} %constant.63.clone) | copy-start | bytes 28
  186.2 12.1 %copy-start.32 = (f32[2]{0:T(128)S(1)}, f32[2]{0:T(128)}, u32[]{:S(2)}) copy-start(f32[2]{0:T(128)} %constant.64.clone) | copy-start | bytes 28
  188.1 6.8 collective-permute-start.26
  191.3 5.3 collective-permute-start.27
  205.6 9.8 %copy-start.5 = (f32[8,2,128,256]{3,0,2,1:T(8,128)}, f32[8,2,128,256]{3,0,2,1:T(8,128)S(1)}, u32[]{:S(2)}) copy-start(f32[8,2,128,256]{3,0,2,1:T(8,128)S(1)} %fusion.182) | copy-start | bytes 6291460
  205.6 8.2 %collective-permute-start.28 = (f32[8,2,1,256]{3,0,2,1:T(8,128)S(1)}, f32[8,2,1,256]{3,0,2,1:T(8,128)S(1)}, u32[]{:S(2)}, u32[]{:S(2)}) collective-permute-start(f32[8,2,1,256]{3,0,2,1:T(8,128)S(1)} %get-tuple-element.47), channel_id=1, source_target_pairs={{32,0},{64,32},{96,64},{128,96},{160,128},{192,160},{224,192},{33,... | collective-permute-start | bytes 49160 | tf_op jit(solution)/shard_map/ppermute | solution.py:18
  206.9 8.4 %collective-permute-start.29 = (f32[8,2,1,256]{3,0,2,1:T(8,128)S(1)}, f32[8,2,1,256]{3,0,2,1:T(8,128)S(1)}, u32[]{:S(2)}, u32[]{:S(2)}) collective-permute-start(f32[8,2,1,256]{3,0,2,1:T(8,128)S(1)} %get-tuple-element.46), channel_id=1, source_target_pairs={{0,32},{32,64},{64,96},{96,128},{128,160},{160,192},{192,224},{1,3... | collective-permute-start | bytes 49160 | tf_op jit(solution)/shard_map/ppermute | solution.py:17
  219.0 7.2 collective-permute-start.30
  222.2 5.7 collective-permute-start.31
  236.5 9.6 %copy-start.6 = (f32[8,2,128,256]{3,0,2,1:T(8,128)}, f32[8,2,128,256]{3,0,2,1:T(8,128)S(1)}, u32[]{:S(2)}) copy-start(f32[8,2,128,256]{3,0,2,1:T(8,128)S(1)} %fusion.183) | copy-start | bytes 6291460
  236.6 8.0 %collective-permute-start.32 = (f32[8,2,1,256]{3,0,2,1:T(8,128)S(1)}, f32[8,2,1,256]{3,0,2,1:T(8,128)S(1)}, u32[]{:S(2)}, u32[]{:S(2)}) collective-permute-start(f32[8,2,1,256]{3,0,2,1:T(8,128)S(1)} %get-tuple-element.45), channel_id=1, source_target_pairs={{32,0},{64,32},{96,64},{128,96},{160,128},{192,160},{224,192},{33,... | collective-permute-start | bytes 49160 | tf_op jit(solution)/shard_map/ppermute | solution.py:18
  237.8 8.1 %collective-permute-start.33 = (f32[8,2,1,256]{3,0,2,1:T(8,128)S(1)}, f32[8,2,1,256]{3,0,2,1:T(8,128)S(1)}, u32[]{:S(2)}, u32[]{:S(2)}) collective-permute-start(f32[8,2,1,256]{3,0,2,1:T(8,128)S(1)} %get-tuple-element.44), channel_id=1, source_target_pairs={{0,32},{32,64},{64,96},{96,128},{128,160},{160,192},{192,224},{1,3... | collective-permute-start | bytes 49160 | tf_op jit(solution)/shard_map/ppermute | solution.py:17
  249.7 7.0 collective-permute-start.34
  252.8 5.5 collective-permute-start.35
  267.0 9.8 %copy-start.7 = (f32[8,2,128,256]{3,0,2,1:T(8,128)}, f32[8,2,128,256]{3,0,2,1:T(8,128)S(1)}, u32[]{:S(2)}) copy-start(f32[8,2,128,256]{3,0,2,1:T(8,128)S(1)} %fusion.184) | copy-start | bytes 6291460
  267.0 8.2 %collective-permute-start.36 = (f32[8,2,1,256]{3,0,2,1:T(8,128)S(1)}, f32[8,2,1,256]{3,0,2,1:T(8,128)S(1)}, u32[]{:S(2)}, u32[]{:S(2)}) collective-permute-start(f32[8,2,1,256]{3,0,2,1:T(8,128)S(1)} %get-tuple-element.43), channel_id=1, source_target_pairs={{32,0},{64,32},{96,64},{128,96},{160,128},{192,160},{224,192},{33,... | collective-permute-start | bytes 49160 | tf_op jit(solution)/shard_map/ppermute | solution.py:18
  268.3 8.4 %collective-permute-start.37 = (f32[8,2,1,256]{3,0,2,1:T(8,128)S(1)}, f32[8,2,1,256]{3,0,2,1:T(8,128)S(1)}, u32[]{:S(2)}, u32[]{:S(2)}) collective-permute-start(f32[8,2,1,256]{3,0,2,1:T(8,128)S(1)} %get-tuple-element.42), channel_id=1, source_target_pairs={{0,32},{32,64},{64,96},{96,128},{128,160},{160,192},{192,224},{1,3... | collective-permute-start | bytes 49160 | tf_op jit(solution)/shard_map/ppermute | solution.py:17
  280.4 7.4 collective-permute-start.38
  283.8 5.7 collective-permute-start.39
  298.2 9.8 %copy-start = (f32[8,2,128,256]{3,0,2,1:T(8,128)}, f32[8,2,128,256]{3,0,2,1:T(8,128)S(1)}, u32[]{:S(2)}) copy-start(f32[8,2,128,256]{3,0,2,1:T(8,128)S(1)} %fusion.185) | copy-start | bytes 6291460
  298.2 8.2 %collective-permute-start.40 = (f32[8,2,1,256]{3,0,2,1:T(8,128)S(1)}, f32[8,2,1,256]{3,0,2,1:T(8,128)S(1)}, u32[]{:S(2)}, u32[]{:S(2)}) collective-permute-start(f32[8,2,1,256]{3,0,2,1:T(8,128)S(1)} %get-tuple-element.41), channel_id=1, source_target_pairs={{32,0},{64,32},{96,64},{128,96},{160,128},{192,160},{224,192},{33,... | collective-permute-start | bytes 49160 | tf_op jit(solution)/shard_map/ppermute | solution.py:18
  299.5 8.4 %collective-permute-start.41 = (f32[8,2,1,256]{3,0,2,1:T(8,128)S(1)}, f32[8,2,1,256]{3,0,2,1:T(8,128)S(1)}, u32[]{:S(2)}, u32[]{:S(2)}) collective-permute-start(f32[8,2,1,256]{3,0,2,1:T(8,128)S(1)} %get-tuple-element.40), channel_id=1, source_target_pairs={{0,32},{32,64},{64,96},{96,128},{128,160},{160,192},{192,224},{1,3... | collective-permute-start | bytes 49160 | tf_op jit(solution)/shard_map/ppermute | solution.py:17
  310.1 16.6 %copy-start.20 = (f32[2,128,256]{2,1,0:T(8,128)S(1)}, f32[2,128,256]{2,1,0:T(8,128)}, u32[]{:S(2)}) copy-start(f32[2,128,256]{2,1,0:T(8,128)} %param.30) | copy-start | bytes 786436
  312.6 9.3 %collective-permute-start.42 = (f32[8,2,130,1]{2,0,3,1:T(8,128)}, f32[8,2,130,1]{2,0,3,1:T(8,128)}, u32[]{:S(2)}, u32[]{:S(2)}) collective-permute-start(f32[8,2,130,1]{2,0,3,1:T(8,128)} %copy.136), channel_id=1, source_target_pairs={{4,0},{8,4},{12,8},{16,12},{20,16},{24,20},{28,24},{5,1},{9,5},{13... | collective-permute-start | bytes 24968 | tf_op jit(solution)/shard_map/ppermute | solution.py:18
  316.4 7.9 %collective-permute-start.43 = (f32[8,2,130,1]{2,0,3,1:T(8,128)}, f32[8,2,130,1]{2,0,3,1:T(8,128)}, u32[]{:S(2)}, u32[]{:S(2)}) collective-permute-start(f32[8,2,130,1]{2,0,3,1:T(8,128)} %copy.138), channel_id=1, source_target_pairs={{0,4},{4,8},{8,12},{12,16},{16,20},{20,24},{24,28},{1,5},{5,9},{9,... | collective-permute-start | bytes 24968 | tf_op jit(solution)/shard_map/ppermute | solution.py:17
  (14 other events, 60.3 us)
Sparse Core Ops, SparseCore 0:
  335.1 99.3 all-gather.1
where the time goes:
time: 752 us; the launch traced here: 741 us
  blocking collectives  280 us (37%)
  starting transfers between devices  137 us (18%)
  waiting for transfers between devices  114 us (15%)
  local copies, waits for them, and re-layouts  103 us (14%)
  other arithmetic  81.4 us (11%)
  between operations  15.5 us (2%)
  matrix products  11 us (1%)
    psum x1, blocking collectives, on_device(): gram_sum = lax.psum(gram_local, ('gx', 'gy'))  280 us
    ppermute x22, starting transfers between devices, with_halo(): before = lax.ppermute(last, axis, up)  108 us
    all_gather x1, waiting for transfers between devices, on_device(): whole = lax.all_gather(own_flat, 'dir', axis=0, tiled=True)  99.5 us
    mul x8, other arithmetic, relax_sweep(): return ice_keep * (state + damping * (source - applied) / diagonal)  51.3 us
    slice x21, local copies, waits for them, and re-layouts, with_halo(): first = lax.slice_in_dim(value, 0, width, axis=dim)  37.7 us
    ppermute x22, starting transfers between devices, with_halo(): after = lax.ppermute(first, axis, down)  28.6 us
    slice x21, local copies, waits for them, and re-layouts, with_halo(): last = lax.slice_in_dim(value, length - width, length, axis=dim)  19.6 us
    ppermute x10, local copies, waits for them, and re-layouts, with_halo(): after = lax.ppermute(first, axis, down)  19.5 us
  transfers between devices with their start and end apart: 45, of which 11 were waited for; matrix products, arithmetic and copies ran while one was open for 6% of the time, Pallas kernels for 0%

commit v1 on v0

--- a/solution.py
+++ b/solution.py
@@ -82,7 +82,7 @@
     gram_local = jnp.dot(
         whole, whole.T, precision=lax.Precision.HIGHEST, preferred_element_type=jnp.float32
     )
-    gram_sum = lax.psum(gram_local, ("gx", "gy"))
+    gram_sum = jnp.sum(lax.all_gather(gram_local, ("gx", "gy")), axis=0)
     lower = jnp.linalg.cholesky(gram_sum / jnp.float32(total_cells))
     inverse = lax.linalg.triangular_solve(lower, identity, left_side=True, lower=True)
     own_rows = lax.dynamic_slice_in_dim(inverse, lax.axis_index("dir") * own_count, own_count, 0)

time: 752 us -> 560 us (0.74)
  the two profiles are of different devices: /device:TPU:64 before, /device:TPU:1 now
where the time goes in v1:
time: 560 us; the launch traced here: 549 us
  starting transfers between devices  145 us (26%)
  local copies, waits for them, and re-layouts  103 us (18%)
  waiting for transfers between devices  99 us (18%)
  blocking collectives  93.9 us (17%)
  other arithmetic  81.5 us (15%)
  between operations  15.6 us (3%)
  matrix products  11 us (2%)
    ppermute x22, starting transfers between devices, with_halo(): before = lax.ppermute(last, axis, up)  106 us
    all_gather x1, blocking collectives, on_device(): gram_sum = jnp.sum(lax.all_gather(gram_local, ('gx', 'gy')), axis=0)  93.9 us
    all_gather x1, waiting for transfers between devices, on_device(): whole = lax.all_gather(own_flat, 'dir', axis=0, tiled=True)  89.7 us
    mul x8, other arithmetic, relax_sweep(): return ice_keep * (state + damping * (source - applied) / diagonal)  51.3 us
    ppermute x22, starting transfers between devices, with_halo(): after = lax.ppermute(first, axis, down)  39 us
    slice x21, local copies, waits for them, and re-layouts, with_halo(): first = lax.slice_in_dim(value, 0, width, axis=dim)  36.5 us
    slice x21, local copies, waits for them, and re-layouts, with_halo(): last = lax.slice_in_dim(value, length - width, length, axis=dim)  20.8 us
    ppermute x10, local copies, waits for them, and re-layouts, with_halo(): after = lax.ppermute(first, axis, down)  19.5 us
  transfers between devices with their start and end apart: 45, of which 12 were waited for; matrix products, arithmetic and copies ran while one was open for 8% of the time, Pallas kernels for 0%

profile of v1, /device:TPU:1, one launch (start us, length us, event | category | flops | bytes accessed | tf_op | source)
XLA Modules:
  0.0 549.3 jit_solution(16831875382917702248)
XLA Ops:
  9.3 4.7 collective-permute-start.1
  16.7 5.0 collective-permute-start.2
  21.7 1.9 collective-permute-start.3
  28.0 4.1 collective-permute-start.5
  37.0 5.0 collective-permute-start.7
  42.7 1.9 collective-permute-start.6
  49.4 7.2 %fusion.4 = f32[8,2,128,256]{3,0,2,1:T(8,128)S(1)} fusion(f32[8,2,128,256]{3,0,2,1:T(8,128)} %copy-done.8, f32[8,2,130,1]{3,0,2,1:T(8,128)} %copy.100, f32[8,2,1,256]{3,0,2,1:T(8,128)S(1)} %collective-permute-done.4, f32[8,2,1,256]{3,0,2,1:T(8,128)} %copy-done.25, f32[8,2,130,1]{3,0,2,1:T(8,128)} %copy.98, f32[128,256]{1,0:T(8,128)S(1)} %get-tuple-element.11, ...), kind=kLoop, calls=%fused_computation.20 | loop fusion | flops 15204352 | bytes 6603024 | tf_op jit(solution)/shard_map/mul | solution.py:41
  58.0 4.5 collective-permute-start.9
  65.6 2.5 copy.101
  68.1 1.9 collective-permute-start.10
  70.0 2.5 copy.103
  72.5 3.7 collective-permute-start.11
  76.2 2.4 copy.102
  78.6 2.3 copy.104
  80.9 5.3 fusion.8
  87.5 4.5 collective-permute-start.13
  95.2 2.6 copy.105
  99.7 2.5 copy.107
  102.2 4.4 collective-permute-start.15
  106.6 2.4 copy.106
  109.0 2.4 copy.108
  111.4 5.3 fusion.12
  118.0 5.7 %collective-permute-start.17 = (f32[8,2,1,256]{3,0,2,1:T(8,128)S(1)}, f32[8,2,1,256]{3,0,2,1:T(8,128)S(1)}, u32[]{:S(2)}, u32[]{:S(2)}) collective-permute-start(f32[8,2,1,256]{3,0,2,1:T(8,128)S(1)} %get-tuple-element.52), channel_id=1, source_target_pairs={{0,32},{32,64},{64,96},{96,128},{128,160},{160,192},{192,224},{1,3... | collective-permute-start | bytes 49160 | tf_op jit(solution)/shard_map/ppermute | solution.py:17
  126.8 2.6 copy.109
  129.4 2.0 collective-permute-start.18
  131.4 2.5 copy.111
  133.9 3.5 collective-permute-start.19
  137.5 2.4 copy.110
  139.8 2.4 copy.112
  142.2 5.3 fusion.16
  148.8 6.7 %collective-permute-start.21 = (f32[8,2,1,256]{3,0,2,1:T(8,128)S(1)}, f32[8,2,1,256]{3,0,2,1:T(8,128)S(1)}, u32[]{:S(2)}, u32[]{:S(2)}) collective-permute-start(f32[8,2,1,256]{3,0,2,1:T(8,128)S(1)} %get-tuple-element.50), channel_id=1, source_target_pairs={{0,32},{32,64},{64,96},{96,128},{128,160},{160,192},{192,224},{1,3... | collective-permute-start | bytes 49160 | tf_op jit(solution)/shard_map/ppermute | solution.py:17
  160.3 2.2 collective-permute-start.22
  163.2 3.5 collective-permute-start.23
  170.1 8.1 %multiply_divide_fusion = (f32[8,2,128,256]{3,0,2,1:T(8,128)S(1)}, f32[8,2,128,256]{3,0,2,1:T(8,128)S(1)}) fusion(f32[2,128,256]{2,1,0:T(8,128)S(1)} %get-tuple-element.69, f32[128,256]{1,0:T(8,128)} %copy-done.17, f32[8,2,128,256]{3,0,2,1:T(8,128)} %copy-done.9, f32[128,256]{1,0:T(8,128)S(1)} %get-tuple-element.11, ...), kind=kLoop, calls=%fused_computation.279 | loop fusion | flops 16777216 | bytes 8962320 | tf_op jit(solution)/shard_map/div | solution.py:46
  179.5 6.7 %collective-permute-start.25 = (f32[8,2,1,256]{3,0,2,1:T(8,128)S(1)}, f32[8,2,1,256]{3,0,2,1:T(8,128)S(1)}, u32[]{:S(2)}, u32[]{:S(2)}) collective-permute-start(f32[8,2,1,256]{3,0,2,1:T(8,128)S(1)} %get-tuple-element.48), channel_id=1, source_target_pairs={{0,32},{32,64},{64,96},{96,128},{128,160},{160,192},{192,224},{1,3... | collective-permute-start | bytes 49160 | tf_op jit(solution)/shard_map/ppermute | solution.py:17
  189.0 1.9 copy.117
  190.9 1.9 collective-permute-start.26
  194.7 4.4 collective-permute-start.27
  202.5 7.3 %fusion.182 = f32[8,2,128,256]{3,0,2,1:T(8,128)S(1)} fusion(f32[8,2,128,256]{3,0,2,1:T(8,128)} %copy-done.10, f32[8,2,128,256]{3,0,2,1:T(8,128)S(1)} %get-tuple-element.13, f32[8,2,1,256]{3,0,2,1:T(8,128)S(1)} %collective-permute-done.24, f32[8,2,1,256]{3,0,2,1:T(8,128)S(1)} %collective-permute-done.25, f32[8,2,130,1]{3,0,2,1:T(8,128)} %copy.120, ...), kind=kLoop, calls=%fused_computation.280 | loop fusion | flops 14680064 | bytes 7389456 | tf_op jit(solution)/shard_map/mul | solution.py:41
  211.2 6.7 %collective-permute-start.29 = (f32[8,2,1,256]{3,0,2,1:T(8,128)S(1)}, f32[8,2,1,256]{3,0,2,1:T(8,128)S(1)}, u32[]{:S(2)}, u32[]{:S(2)}) collective-permute-start(f32[8,2,1,256]{3,0,2,1:T(8,128)S(1)} %get-tuple-element.46), channel_id=1, source_target_pairs={{0,32},{32,64},{64,96},{96,128},{128,160},{160,192},{192,224},{1,3... | collective-permute-start | bytes 49160 | tf_op jit(solution)/shard_map/ppermute | solution.py:17
  222.4 1.9 collective-permute-start.30
  226.2 4.0 collective-permute-start.31
  233.6 7.0 %fusion.183 = f32[8,2,128,256]{3,0,2,1:T(8,128)S(1)} fusion(f32[8,2,128,256]{3,0,2,1:T(8,128)} %copy-done.5, f32[8,2,128,256]{3,0,2,1:T(8,128)S(1)} %get-tuple-element.13, f32[8,2,1,256]{3,0,2,1:T(8,128)S(1)} %collective-permute-done.28, f32[8,2,1,256]{3,0,2,1:T(8,128)S(1)} %collective-permute-done.29, f32[8,2,130,1]{3,0,2,1:T(8,128)} %copy.124, ...), kind=kLoop, calls=%fused_computation.281 | loop fusion | flops 14680064 | bytes 7389456 | tf_op jit(solution)/shard_map/mul | solution.py:41
  241.9 6.4 %collective-permute-start.33 = (f32[8,2,1,256]{3,0,2,1:T(8,128)S(1)}, f32[8,2,1,256]{3,0,2,1:T(8,128)S(1)}, u32[]{:S(2)}, u32[]{:S(2)}) collective-permute-start(f32[8,2,1,256]{3,0,2,1:T(8,128)S(1)} %get-tuple-element.44), channel_id=1, source_target_pairs={{0,32},{32,64},{64,96},{96,128},{128,160},{160,192},{192,224},{1,3... | collective-permute-start | bytes 49160 | tf_op jit(solution)/shard_map/ppermute | solution.py:17
  252.9 1.9 collective-permute-start.34
  256.7 4.2 collective-permute-start.35
  264.3 7.0 %fusion.184 = f32[8,2,128,256]{3,0,2,1:T(8,128)S(1)} fusion(f32[8,2,128,256]{3,0,2,1:T(8,128)} %copy-done.6, f32[8,2,128,256]{3,0,2,1:T(8,128)S(1)} %get-tuple-element.13, f32[8,2,1,256]{3,0,2,1:T(8,128)S(1)} %collective-permute-done.32, f32[8,2,1,256]{3,0,2,1:T(8,128)S(1)} %collective-permute-done.33, f32[8,2,130,1]{3,0,2,1:T(8,128)} %copy.128, ...), kind=kLoop, calls=%fused_computation.282 | loop fusion | flops 14680064 | bytes 7389456 | tf_op jit(solution)/shard_map/mul | solution.py:41
  272.6 6.7 %collective-permute-start.37 = (f32[8,2,1,256]{3,0,2,1:T(8,128)S(1)}, f32[8,2,1,256]{3,0,2,1:T(8,128)S(1)}, u32[]{:S(2)}, u32[]{:S(2)}) collective-permute-start(f32[8,2,1,256]{3,0,2,1:T(8,128)S(1)} %get-tuple-element.42), channel_id=1, source_target_pairs={{0,32},{32,64},{64,96},{96,128},{128,160},{160,192},{192,224},{1,3... | collective-permute-start | bytes 49160 | tf_op jit(solution)/shard_map/ppermute | solution.py:17
  283.8 2.1 collective-permute-start.38
  287.8 4.2 collective-permute-start.39
  295.4 7.0 %fusion.185 = f32[8,2,128,256]{3,0,2,1:T(8,128)S(1)} fusion(f32[8,2,128,256]{3,0,2,1:T(8,128)} %copy-done.7, f32[8,2,128,256]{3,0,2,1:T(8,128)S(1)} %get-tuple-element.13, f32[8,2,1,256]{3,0,2,1:T(8,128)S(1)} %collective-permute-done.36, f32[8,2,1,256]{3,0,2,1:T(8,128)S(1)} %collective-permute-done.37, f32[8,2,130,1]{3,0,2,1:T(8,128)} %copy.132, ...), kind=kLoop, calls=%fused_computation.283 | loop fusion | flops 14680064 | bytes 7389456 | tf_op jit(solution)/shard_map/mul | solution.py:41
  303.7 6.7 %collective-permute-start.41 = (f32[8,2,1,256]{3,0,2,1:T(8,128)S(1)}, f32[8,2,1,256]{3,0,2,1:T(8,128)S(1)}, u32[]{:S(2)}, u32[]{:S(2)}) collective-permute-start(f32[8,2,1,256]{3,0,2,1:T(8,128)S(1)} %get-tuple-element.40), channel_id=1, source_target_pairs={{0,32},{32,64},{64,96},{96,128},{128,160},{160,192},{192,224},{1,3... | collective-permute-start | bytes 49160 | tf_op jit(solution)/shard_map/ppermute | solution.py:17
  313.5 2.5 copy.133
  317.9 2.5 copy.135
  320.4 4.2 collective-permute-start.43
  325.6 2.4 copy.134
  328.0 2.4 copy.136
  330.3 7.1 %multiply_reduce_fusion = f32[8,128,256]{2,0,1:T(8,128)S(1)} fusion(f32[8,2,128,256]{3,0,2,1:T(8,128)} %copy-done, f32[8,2,128,256]{3,0,2,1:T(8,128)S(1)} %get-tuple-element.13, f32[8,2,1,256]{3,0,2,1:T(8,128)S(1)} %collective-permute-done.40, f32[8,2,1,256]{3,0,2,1:T(8,128)} %copy-done.23, f32[8,2,130,1]{3,0,2,1:T(8,128)} %copy.136, ...), kind=kLoop, calls=%fused_computation.278 | loop fusion | flops 15466496 | bytes 6603024 | tf_op jit(solution)/shard_map/reduce_sum | solution.py:76
  338.6 89.7 %all-gather.3.cloned.1.call-done = f32[32,32768]{1,0:T(8,128)} async-done(((f32[8,32768]{1,0:T(8,128)}), f32[32,32768]{1,0:T(8,128)}) %all-gather.3.cloned.1.call-update) | async-done | bytes 4194320 | tf_op jit(solution)/shard_map/all_gather | solution.py:81
  428.3 6.9 %fusion.230 = f32[32,32]{1,0:T(8,128)S(1)} fusion(f32[32,32768]{1,0:T(8,128)} %all-gather.3.cloned.1.call-done), kind=kOutput, calls=%fused_computation.345 | convolution fusion | flops 402653184 | bytes 4198400 | tf_op jit(solution)/shard_map/dot_general | solution.py:82
  435.3 93.9 %all-gather = f32[2048,32]{1,0:T(8,128)S(1)} all-gather(f32[32,32]{1,0:T(8,128)S(1)} %fusion.230), channel_id=2, replica_groups=mesh['gx'=8,'gy'=8,'dir'=4] {'gx','gy'}, dimensions={0}, use_global_device_ids=true | all-gather | bytes 266240 | tf_op jit(solution)/shard_map/all_gather | solution.py:85
  529.3 2.9 cholesky.17
  533.6 2.4 custom-call.6
  536.2 3.8 fusion.198
  (200 shorter events, 99.1 us)
Async XLA Ops:
  7.2 18.1 %copy-start.21 = (f32[128,256]{1,0:T(8,128)S(1)}, f32[128,256]{1,0:T(8,128)}, u32[]{:S(2)}) copy-start(f32[128,256]{1,0:T(8,128)} %param.31) | copy-start | bytes 393220
  7.2 17.4 %copy-start.18 = (f32[8,128,256]{2,1,0:T(8,128)S(1)}, f32[8,128,256]{2,1,0:T(8,128)}, u32[]{:S(2)}) copy-start(f32[8,128,256]{2,1,0:T(8,128)} %param.29) | copy-start | bytes 3145732
  7.2 421.1 %all-gather.3.cloned.1.call-start = ((), (), s32[]{:S(2)}) async-start(), calls=%async_computation | async-start | bytes 5242880 | tf_op jit(solution)/shard_map/all_gather | solution.py:81
  8.0 7.6 %collective-permute-start = (f32[1,256]{1,0:T(1,128)S(1)}, f32[1,256]{1,0:T(1,128)S(1)}, u32[]{:S(2)}, u32[]{:S(2)}) collective-permute-start(f32[1,256]{1,0:T(1,128)S(1)} %get-tuple-element.66), channel_id=1, source_target_pairs={{32,0},{64,32},{96,64},{128,96},{160,128},{192,160},{224,192},{33,... | collective-permute-start | bytes 3080 | tf_op jit(solution)/shard_map/ppermute | solution.py:18
  9.3 6.3 %collective-permute-start.1 = (f32[1,256]{1,0:T(1,128)S(1)}, f32[1,256]{1,0:T(1,128)S(1)}, u32[]{:S(2)}, u32[]{:S(2)}) collective-permute-start(f32[1,256]{1,0:T(1,128)S(1)} %get-tuple-element.65), channel_id=1, source_target_pairs={{0,32},{32,64},{64,96},{96,128},{128,160},{160,192},{192,224},{1,3... | collective-permute-start | bytes 3080 | tf_op jit(solution)/shard_map/ppermute | solution.py:17
  15.6 10.6 %copy-start.19 = (f32[2,128,256]{2,1,0:T(8,128)S(1)}, f32[2,128,256]{2,1,0:T(8,128)}, u32[]{:S(2)}) copy-start(f32[2,128,256]{2,1,0:T(8,128)} %param.30) | copy-start | bytes 786436
  15.6 10.6 %copy-start.29 = (f32[2]{0:T(128)S(1)}, f32[2]{0:T(128)}, u32[]{:S(2)}) copy-start(f32[2]{0:T(128)} %constant.64.clone) | copy-start | bytes 28
  15.6 10.6 %copy-start.31 = (f32[2]{0:T(128)S(1)}, f32[2]{0:T(128)}, u32[]{:S(2)}) copy-start(f32[2]{0:T(128)} %constant.65.clone) | copy-start | bytes 28
  16.7 8.6 %collective-permute-start.2 = (f32[130,1]{1,0:T(8,128)S(1)}, f32[130,1]{1,0:T(8,128)S(1)}, u32[]{:S(2)}, u32[]{:S(2)}) collective-permute-start(f32[130,1]{1,0:T(8,128)S(1)} %get-tuple-element.60), channel_id=1, source_target_pairs={{4,0},{8,4},{12,8},{16,12},{20,16},{24,20},{28,24},{5,1},{9,5},{13... | collective-permute-start | bytes 1568 | tf_op jit(solution)/shard_map/ppermute | solution.py:18
  21.7 3.5 collective-permute-start.3
  26.7 5.4 collective-permute-start.4
  28.0 5.0 collective-permute-start.5
  35.1 9.5 %copy-start.22 = (s32[128,256]{1,0:T(8,128)S(1)}, s32[128,256]{1,0:T(8,128)}, u32[]{:S(2)}) copy-start(s32[128,256]{1,0:T(8,128)} %param.34) | copy-start | bytes 393220
  37.0 8.3 %collective-permute-start.7 = (f32[8,2,130,1]{2,0,3,1:T(8,128)S(1)}, f32[8,2,130,1]{2,0,3,1:T(8,128)S(1)}, u32[]{:S(2)}, u32[]{:S(2)}) collective-permute-start(f32[8,2,130,1]{2,0,3,1:T(8,128)S(1)} %copy.99), channel_id=1, source_target_pairs={{0,4},{4,8},{8,12},{12,16},{16,20},{20,24},{24,28},{1,5},{5,9},{9,... | collective-permute-start | bytes 24968 | tf_op jit(solution)/shard_map/ppermute | solution.py:17
  42.7 5.1 collective-permute-start.6
  56.7 5.9 %collective-permute-start.8 = (f32[8,2,1,256]{3,0,2,1:T(8,128)S(1)}, f32[8,2,1,256]{3,0,2,1:T(8,128)S(1)}, u32[]{:S(2)}, u32[]{:S(2)}) collective-permute-start(f32[8,2,1,256]{3,0,2,1:T(8,128)S(1)} %get-tuple-element.57), channel_id=1, source_target_pairs={{32,0},{64,32},{96,64},{128,96},{160,128},{192,160},{224,192},{33,... | collective-permute-start | bytes 49160 | tf_op jit(solution)/shard_map/ppermute | solution.py:18
  58.0 5.4 collective-permute-start.9
  68.1 8.1 %collective-permute-start.10 = (f32[8,2,130,1]{2,0,3,1:T(8,128)}, f32[8,2,130,1]{2,0,3,1:T(8,128)}, u32[]{:S(2)}, u32[]{:S(2)}) collective-permute-start(f32[8,2,130,1]{2,0,3,1:T(8,128)} %copy.101), channel_id=1, source_target_pairs={{4,0},{8,4},{12,8},{16,12},{20,16},{24,20},{28,24},{5,1},{9,5},{13... | collective-permute-start | bytes 24968 | tf_op jit(solution)/shard_map/ppermute | solution.py:18
  72.5 6.1 %collective-permute-start.11 = (f32[8,2,130,1]{2,0,3,1:T(8,128)}, f32[8,2,130,1]{2,0,3,1:T(8,128)}, u32[]{:S(2)}, u32[]{:S(2)}) collective-permute-start(f32[8,2,130,1]{2,0,3,1:T(8,128)} %copy.103), channel_id=1, source_target_pairs={{0,4},{4,8},{8,12},{12,16},{16,20},{20,24},{24,28},{1,5},{5,9},{9,... | collective-permute-start | bytes 24968 | tf_op jit(solution)/shard_map/ppermute | solution.py:17
  86.2 5.9 %collective-permute-start.12 = (f32[8,2,1,256]{3,0,2,1:T(8,128)S(1)}, f32[8,2,1,256]{3,0,2,1:T(8,128)S(1)}, u32[]{:S(2)}, u32[]{:S(2)}) collective-permute-start(f32[8,2,1,256]{3,0,2,1:T(8,128)S(1)} %get-tuple-element.55), channel_id=1, source_target_pairs={{32,0},{64,32},{96,64},{128,96},{160,128},{192,160},{224,192},{33,... | collective-permute-start | bytes 49160 | tf_op jit(solution)/shard_map/ppermute | solution.py:18
  87.5 5.4 collective-permute-start.13
  95.2 16.2 %copy-start.2 = (f32[8,2,128,256]{3,0,2,1:T(8,128)S(1)}, f32[8,2,128,256]{3,0,2,1:T(8,128)}, u32[]{:S(2)}) copy-start(f32[8,2,128,256]{3,0,2,1:T(8,128)} %copy-done.1) | copy-start | bytes 6291460
  97.8 8.8 %collective-permute-start.14 = (f32[8,2,130,1]{2,0,3,1:T(8,128)}, f32[8,2,130,1]{2,0,3,1:T(8,128)}, u32[]{:S(2)}, u32[]{:S(2)}) collective-permute-start(f32[8,2,130,1]{2,0,3,1:T(8,128)} %copy.105), channel_id=1, source_target_pairs={{4,0},{8,4},{12,8},{16,12},{20,16},{24,20},{28,24},{5,1},{9,5},{13... | collective-permute-start | bytes 24968 | tf_op jit(solution)/shard_map/ppermute | solution.py:18
  102.2 6.8 %collective-permute-start.15 = (f32[8,2,130,1]{2,0,3,1:T(8,128)}, f32[8,2,130,1]{2,0,3,1:T(8,128)}, u32[]{:S(2)}, u32[]{:S(2)}) collective-permute-start(f32[8,2,130,1]{2,0,3,1:T(8,128)} %copy.107), channel_id=1, source_target_pairs={{0,4},{4,8},{8,12},{12,16},{16,20},{20,24},{24,28},{1,5},{5,9},{9,... | collective-permute-start | bytes 24968 | tf_op jit(solution)/shard_map/ppermute | solution.py:17
  116.7 7.0 %collective-permute-start.16 = (f32[8,2,1,256]{3,0,2,1:T(8,128)S(1)}, f32[8,2,1,256]{3,0,2,1:T(8,128)S(1)}, u32[]{:S(2)}, u32[]{:S(2)}) collective-permute-start(f32[8,2,1,256]{3,0,2,1:T(8,128)S(1)} %get-tuple-element.53), channel_id=1, source_target_pairs={{32,0},{64,32},{96,64},{128,96},{160,128},{192,160},{224,192},{33,... | collective-permute-start | bytes 49160 | tf_op jit(solution)/shard_map/ppermute | solution.py:18
  118.0 6.5 %collective-permute-start.17 = (f32[8,2,1,256]{3,0,2,1:T(8,128)S(1)}, f32[8,2,1,256]{3,0,2,1:T(8,128)S(1)}, u32[]{:S(2)}, u32[]{:S(2)}) collective-permute-start(f32[8,2,1,256]{3,0,2,1:T(8,128)S(1)} %get-tuple-element.52), channel_id=1, source_target_pairs={{0,32},{32,64},{64,96},{96,128},{128,160},{160,192},{192,224},{1,3... | collective-permute-start | bytes 49160 | tf_op jit(solution)/shard_map/ppermute | solution.py:17
  126.8 15.4 %copy-start.4 = (f32[8,2,128,256]{3,0,2,1:T(8,128)S(1)}, f32[8,2,128,256]{3,0,2,1:T(8,128)}, u32[]{:S(2)}) copy-start(f32[8,2,128,256]{3,0,2,1:T(8,128)} %copy-done.3) | copy-start | bytes 6291460
  129.4 8.0 %collective-permute-start.18 = (f32[8,2,130,1]{2,0,3,1:T(8,128)}, f32[8,2,130,1]{2,0,3,1:T(8,128)}, u32[]{:S(2)}, u32[]{:S(2)}) collective-permute-start(f32[8,2,130,1]{2,0,3,1:T(8,128)} %copy.109), channel_id=1, source_target_pairs={{4,0},{8,4},{12,8},{16,12},{20,16},{24,20},{28,24},{5,1},{9,5},{13... | collective-permute-start | bytes 24968 | tf_op jit(solution)/shard_map/ppermute | solution.py:18
  133.9 5.9 %collective-permute-start.19 = (f32[8,2,130,1]{2,0,3,1:T(8,128)}, f32[8,2,130,1]{2,0,3,1:T(8,128)}, u32[]{:S(2)}, u32[]{:S(2)}) collective-permute-start(f32[8,2,130,1]{2,0,3,1:T(8,128)} %copy.111), channel_id=1, source_target_pairs={{0,4},{4,8},{8,12},{12,16},{16,20},{20,24},{24,28},{1,5},{5,9},{9,... | collective-permute-start | bytes 24968 | tf_op jit(solution)/shard_map/ppermute | solution.py:17
  147.5 9.6 %copy-start.9 = (f32[8,2,128,256]{3,0,2,1:T(8,128)}, f32[8,2,128,256]{3,0,2,1:T(8,128)S(1)}, u32[]{:S(2)}) copy-start(f32[8,2,128,256]{3,0,2,1:T(8,128)S(1)} %fusion.16) | copy-start | bytes 6291460
  147.5 8.0 %collective-permute-start.20 = (f32[8,2,1,256]{3,0,2,1:T(8,128)S(1)}, f32[8,2,1,256]{3,0,2,1:T(8,128)S(1)}, u32[]{:S(2)}, u32[]{:S(2)}) collective-permute-start(f32[8,2,1,256]{3,0,2,1:T(8,128)S(1)} %get-tuple-element.51), channel_id=1, source_target_pairs={{32,0},{64,32},{96,64},{128,96},{160,128},{192,160},{224,192},{33,... | collective-permute-start | bytes 49160 | tf_op jit(solution)/shard_map/ppermute | solution.py:18
  148.8 7.5 %collective-permute-start.21 = (f32[8,2,1,256]{3,0,2,1:T(8,128)S(1)}, f32[8,2,1,256]{3,0,2,1:T(8,128)S(1)}, u32[]{:S(2)}, u32[]{:S(2)}) collective-permute-start(f32[8,2,1,256]{3,0,2,1:T(8,128)S(1)} %get-tuple-element.50), channel_id=1, source_target_pairs={{0,32},{32,64},{64,96},{96,128},{128,160},{160,192},{192,224},{1,3... | collective-permute-start | bytes 49160 | tf_op jit(solution)/shard_map/ppermute | solution.py:17
  160.3 6.4 %collective-permute-start.22 = (f32[8,2,130,1]{2,0,3,1:T(8,128)S(1)}, f32[8,2,130,1]{2,0,3,1:T(8,128)S(1)}, u32[]{:S(2)}, u32[]{:S(2)}) collective-permute-start(f32[8,2,130,1]{2,0,3,1:T(8,128)S(1)} %copy.113), channel_id=1, source_target_pairs={{4,0},{8,4},{12,8},{16,12},{20,16},{24,20},{28,24},{5,1},{9,5},{13... | collective-permute-start | bytes 24968 | tf_op jit(solution)/shard_map/ppermute | solution.py:18
  163.2 5.2 collective-permute-start.23
  178.2 9.0 %copy-start.10 = (f32[8,2,128,256]{3,0,2,1:T(8,128)}, f32[8,2,128,256]{3,0,2,1:T(8,128)S(1)}, u32[]{:S(2)}) copy-start(f32[8,2,128,256]{3,0,2,1:T(8,128)S(1)} %get-tuple-element.12) | copy-start | bytes 6291460
  178.2 8.0 %collective-permute-start.24 = (f32[8,2,1,256]{3,0,2,1:T(8,128)S(1)}, f32[8,2,1,256]{3,0,2,1:T(8,128)S(1)}, u32[]{:S(2)}, u32[]{:S(2)}) collective-permute-start(f32[8,2,1,256]{3,0,2,1:T(8,128)S(1)} %get-tuple-element.49), channel_id=1, source_target_pairs={{32,0},{64,32},{96,64},{128,96},{160,128},{192,160},{224,192},{33,... | collective-permute-start | bytes 49160 | tf_op jit(solution)/shard_map/ppermute | solution.py:18
  179.5 7.5 %collective-permute-start.25 = (f32[8,2,1,256]{3,0,2,1:T(8,128)S(1)}, f32[8,2,1,256]{3,0,2,1:T(8,128)S(1)}, u32[]{:S(2)}, u32[]{:S(2)}) collective-permute-start(f32[8,2,1,256]{3,0,2,1:T(8,128)S(1)} %get-tuple-element.48), channel_id=1, source_target_pairs={{0,32},{32,64},{64,96},{96,128},{128,160},{160,192},{192,224},{1,3... | collective-permute-start | bytes 49160 | tf_op jit(solution)/shard_map/ppermute | solution.py:17
  188.9 13.5 %copy-start.11 = (f32[128,256]{1,0:T(8,128)S(1)}, f32[128,256]{1,0:T(8,128)}, u32[]{:S(2)}) copy-start(f32[128,256]{1,0:T(8,128)} %convert_element_type.8) | copy-start | bytes 393220
  188.9 13.5 %copy-start.12 = (f32[128,256]{1,0:T(8,128)S(1)}, f32[128,256]{1,0:T(8,128)}, u32[]{:S(2)}) copy-start(f32[128,256]{1,0:T(8,128)} %get-tuple-element.15) | copy-start | bytes 393220
  188.9 13.5 %copy-start.13 = (f32[128,256]{1,0:T(8,128)S(1)}, f32[128,256]{1,0:T(8,128)}, u32[]{:S(2)}) copy-start(f32[128,256]{1,0:T(8,128)} %get-tuple-element.16) | copy-start | bytes 393220
  188.9 13.5 %copy-start.14 = (f32[128,256]{1,0:T(8,128)S(1)}, f32[128,256]{1,0:T(8,128)}, u32[]{:S(2)}) copy-start(f32[128,256]{1,0:T(8,128)} %get-tuple-element.63) | copy-start | bytes 393220
  188.9 13.5 %copy-start.15 = (f32[128,256]{1,0:T(8,128)S(1)}, f32[128,256]{1,0:T(8,128)}, u32[]{:S(2)}) copy-start(f32[128,256]{1,0:T(8,128)} %get-tuple-element.64) | copy-start | bytes 393220
  189.0 13.5 %copy-start.30 = (f32[2]{0:T(128)S(1)}, f32[2]{0:T(128)}, u32[]{:S(2)}) copy-start(f32[2]{0:T(128)} %constant.64.clone) | copy-start | bytes 28
  189.0 13.5 %copy-start.32 = (f32[2]{0:T(128)S(1)}, f32[2]{0:T(128)}, u32[]{:S(2)}) copy-start(f32[2]{0:T(128)} %constant.65.clone) | copy-start | bytes 28
  190.9 8.2 %collective-permute-start.26 = (f32[8,2,130,1]{2,0,3,1:T(8,128)S(1)}, f32[8,2,130,1]{2,0,3,1:T(8,128)S(1)}, u32[]{:S(2)}, u32[]{:S(2)}) collective-permute-start(f32[8,2,130,1]{2,0,3,1:T(8,128)S(1)} %copy.117), channel_id=1, source_target_pairs={{4,0},{8,4},{12,8},{16,12},{20,16},{24,20},{28,24},{5,1},{9,5},{13... | collective-permute-start | bytes 24968 | tf_op jit(solution)/shard_map/ppermute | solution.py:18
  194.7 6.1 %collective-permute-start.27 = (f32[8,2,130,1]{2,0,3,1:T(8,128)S(1)}, f32[8,2,130,1]{2,0,3,1:T(8,128)S(1)}, u32[]{:S(2)}, u32[]{:S(2)}) collective-permute-start(f32[8,2,130,1]{2,0,3,1:T(8,128)S(1)} %copy.119), channel_id=1, source_target_pairs={{0,4},{4,8},{8,12},{12,16},{16,20},{20,24},{24,28},{1,5},{5,9},{9,... | collective-permute-start | bytes 24968 | tf_op jit(solution)/shard_map/ppermute | solution.py:17
  209.9 8.0 %collective-permute-start.28 = (f32[8,2,1,256]{3,0,2,1:T(8,128)S(1)}, f32[8,2,1,256]{3,0,2,1:T(8,128)S(1)}, u32[]{:S(2)}, u32[]{:S(2)}) collective-permute-start(f32[8,2,1,256]{3,0,2,1:T(8,128)S(1)} %get-tuple-element.47), channel_id=1, source_target_pairs={{32,0},{64,32},{96,64},{128,96},{160,128},{192,160},{224,192},{33,... | collective-permute-start | bytes 49160 | tf_op jit(solution)/shard_map/ppermute | solution.py:18
  211.2 7.5 %collective-permute-start.29 = (f32[8,2,1,256]{3,0,2,1:T(8,128)S(1)}, f32[8,2,1,256]{3,0,2,1:T(8,128)S(1)}, u32[]{:S(2)}, u32[]{:S(2)}) collective-permute-start(f32[8,2,1,256]{3,0,2,1:T(8,128)S(1)} %get-tuple-element.46), channel_id=1, source_target_pairs={{0,32},{32,64},{64,96},{96,128},{128,160},{160,192},{192,224},{1,3... | collective-permute-start | bytes 49160 | tf_op jit(solution)/shard_map/ppermute | solution.py:17
  222.4 7.9 %collective-permute-start.30 = (f32[8,2,130,1]{2,0,3,1:T(8,128)S(1)}, f32[8,2,130,1]{2,0,3,1:T(8,128)S(1)}, u32[]{:S(2)}, u32[]{:S(2)}) collective-permute-start(f32[8,2,130,1]{2,0,3,1:T(8,128)S(1)} %copy.121), channel_id=1, source_target_pairs={{4,0},{8,4},{12,8},{16,12},{20,16},{24,20},{28,24},{5,1},{9,5},{13... | collective-permute-start | bytes 24968 | tf_op jit(solution)/shard_map/ppermute | solution.py:18
  226.2 5.8 %collective-permute-start.31 = (f32[8,2,130,1]{2,0,3,1:T(8,128)S(1)}, f32[8,2,130,1]{2,0,3,1:T(8,128)S(1)}, u32[]{:S(2)}, u32[]{:S(2)}) collective-permute-start(f32[8,2,130,1]{2,0,3,1:T(8,128)S(1)} %copy.123), channel_id=1, source_target_pairs={{0,4},{4,8},{8,12},{12,16},{16,20},{20,24},{24,28},{1,5},{5,9},{9,... | collective-permute-start | bytes 24968 | tf_op jit(solution)/shard_map/ppermute | solution.py:17
  240.6 7.7 %collective-permute-start.32 = (f32[8,2,1,256]{3,0,2,1:T(8,128)S(1)}, f32[8,2,1,256]{3,0,2,1:T(8,128)S(1)}, u32[]{:S(2)}, u32[]{:S(2)}) collective-permute-start(f32[8,2,1,256]{3,0,2,1:T(8,128)S(1)} %get-tuple-element.45), channel_id=1, source_target_pairs={{32,0},{64,32},{96,64},{128,96},{160,128},{192,160},{224,192},{33,... | collective-permute-start | bytes 49160 | tf_op jit(solution)/shard_map/ppermute | solution.py:18
  241.9 7.3 %collective-permute-start.33 = (f32[8,2,1,256]{3,0,2,1:T(8,128)S(1)}, f32[8,2,1,256]{3,0,2,1:T(8,128)S(1)}, u32[]{:S(2)}, u32[]{:S(2)}) collective-permute-start(f32[8,2,1,256]{3,0,2,1:T(8,128)S(1)} %get-tuple-element.44), channel_id=1, source_target_pairs={{0,32},{32,64},{64,96},{96,128},{128,160},{160,192},{192,224},{1,3... | collective-permute-start | bytes 49160 | tf_op jit(solution)/shard_map/ppermute | solution.py:17
  252.9 8.0 %collective-permute-start.34 = (f32[8,2,130,1]{2,0,3,1:T(8,128)S(1)}, f32[8,2,130,1]{2,0,3,1:T(8,128)S(1)}, u32[]{:S(2)}, u32[]{:S(2)}) collective-permute-start(f32[8,2,130,1]{2,0,3,1:T(8,128)S(1)} %copy.125), channel_id=1, source_target_pairs={{4,0},{8,4},{12,8},{16,12},{20,16},{24,20},{28,24},{5,1},{9,5},{13... | collective-permute-start | bytes 24968 | tf_op jit(solution)/shard_map/ppermute | solution.py:18
  256.7 5.9 %collective-permute-start.35 = (f32[8,2,130,1]{2,0,3,1:T(8,128)S(1)}, f32[8,2,130,1]{2,0,3,1:T(8,128)S(1)}, u32[]{:S(2)}, u32[]{:S(2)}) collective-permute-start(f32[8,2,130,1]{2,0,3,1:T(8,128)S(1)} %copy.127), channel_id=1, source_target_pairs={{0,4},{4,8},{8,12},{12,16},{16,20},{20,24},{24,28},{1,5},{5,9},{9,... | collective-permute-start | bytes 24968 | tf_op jit(solution)/shard_map/ppermute | solution.py:17
  271.3 8.0 %collective-permute-start.36 = (f32[8,2,1,256]{3,0,2,1:T(8,128)S(1)}, f32[8,2,1,256]{3,0,2,1:T(8,128)S(1)}, u32[]{:S(2)}, u32[]{:S(2)}) collective-permute-start(f32[8,2,1,256]{3,0,2,1:T(8,128)S(1)} %get-tuple-element.43), channel_id=1, source_target_pairs={{32,0},{64,32},{96,64},{128,96},{160,128},{192,160},{224,192},{33,... | collective-permute-start | bytes 49160 | tf_op jit(solution)/shard_map/ppermute | solution.py:18
  272.6 7.5 %collective-permute-start.37 = (f32[8,2,1,256]{3,0,2,1:T(8,128)S(1)}, f32[8,2,1,256]{3,0,2,1:T(8,128)S(1)}, u32[]{:S(2)}, u32[]{:S(2)}) collective-permute-start(f32[8,2,1,256]{3,0,2,1:T(8,128)S(1)} %get-tuple-element.42), channel_id=1, source_target_pairs={{0,32},{32,64},{64,96},{96,128},{128,160},{160,192},{192,224},{1,3... | collective-permute-start | bytes 49160 | tf_op jit(solution)/shard_map/ppermute | solution.py:17
  283.8 8.2 %collective-permute-start.38 = (f32[8,2,130,1]{2,0,3,1:T(8,128)S(1)}, f32[8,2,130,1]{2,0,3,1:T(8,128)S(1)}, u32[]{:S(2)}, u32[]{:S(2)}) collective-permute-start(f32[8,2,130,1]{2,0,3,1:T(8,128)S(1)} %copy.129), channel_id=1, source_target_pairs={{4,0},{8,4},{12,8},{16,12},{20,16},{24,20},{28,24},{5,1},{9,5},{13... | collective-permute-start | bytes 24968 | tf_op jit(solution)/shard_map/ppermute | solution.py:18
  287.8 5.9 %collective-permute-start.39 = (f32[8,2,130,1]{2,0,3,1:T(8,128)S(1)}, f32[8,2,130,1]{2,0,3,1:T(8,128)S(1)}, u32[]{:S(2)}, u32[]{:S(2)}) collective-permute-start(f32[8,2,130,1]{2,0,3,1:T(8,128)S(1)} %copy.131), channel_id=1, source_target_pairs={{0,4},{4,8},{8,12},{12,16},{16,20},{20,24},{24,28},{1,5},{5,9},{9,... | collective-permute-start | bytes 24968 | tf_op jit(solution)/shard_map/ppermute | solution.py:17
  302.4 9.0 %copy-start = (f32[8,2,128,256]{3,0,2,1:T(8,128)}, f32[8,2,128,256]{3,0,2,1:T(8,128)S(1)}, u32[]{:S(2)}) copy-start(f32[8,2,128,256]{3,0,2,1:T(8,128)S(1)} %fusion.185) | copy-start | bytes 6291460
  302.4 8.0 %collective-permute-start.40 = (f32[8,2,1,256]{3,0,2,1:T(8,128)S(1)}, f32[8,2,1,256]{3,0,2,1:T(8,128)S(1)}, u32[]{:S(2)}, u32[]{:S(2)}) collective-permute-start(f32[8,2,1,256]{3,0,2,1:T(8,128)S(1)} %get-tuple-element.41), channel_id=1, source_target_pairs={{32,0},{64,32},{96,64},{128,96},{160,128},{192,160},{224,192},{33,... | collective-permute-start | bytes 49160 | tf_op jit(solution)/shard_map/ppermute | solution.py:18
  303.7 7.5 %collective-permute-start.41 = (f32[8,2,1,256]{3,0,2,1:T(8,128)S(1)}, f32[8,2,1,256]{3,0,2,1:T(8,128)S(1)}, u32[]{:S(2)}, u32[]{:S(2)}) collective-permute-start(f32[8,2,1,256]{3,0,2,1:T(8,128)S(1)} %get-tuple-element.40), channel_id=1, source_target_pairs={{0,32},{32,64},{64,96},{96,128},{128,160},{160,192},{192,224},{1,3... | collective-permute-start | bytes 49160 | tf_op jit(solution)/shard_map/ppermute | solution.py:17
  313.5 16.8 %copy-start.20 = (f32[2,128,256]{2,1,0:T(8,128)S(1)}, f32[2,128,256]{2,1,0:T(8,128)}, u32[]{:S(2)}) copy-start(f32[2,128,256]{2,1,0:T(8,128)} %param.30) | copy-start | bytes 786436
  316.0 9.6 %collective-permute-start.42 = (f32[8,2,130,1]{2,0,3,1:T(8,128)}, f32[8,2,130,1]{2,0,3,1:T(8,128)}, u32[]{:S(2)}, u32[]{:S(2)}) collective-permute-start(f32[8,2,130,1]{2,0,3,1:T(8,128)} %copy.133), channel_id=1, source_target_pairs={{4,0},{8,4},{12,8},{16,12},{20,16},{24,20},{28,24},{5,1},{9,5},{13... | collective-permute-start | bytes 24968 | tf_op jit(solution)/shard_map/ppermute | solution.py:18
  320.4 7.6 %collective-permute-start.43 = (f32[8,2,130,1]{2,0,3,1:T(8,128)}, f32[8,2,130,1]{2,0,3,1:T(8,128)}, u32[]{:S(2)}, u32[]{:S(2)}) collective-permute-start(f32[8,2,130,1]{2,0,3,1:T(8,128)} %copy.135), channel_id=1, source_target_pairs={{0,4},{4,8},{8,12},{12,16},{16,20},{20,24},{24,28},{1,5},{5,9},{9,... | collective-permute-start | bytes 24968 | tf_op jit(solution)/shard_map/ppermute | solution.py:17
  (14 other events, 61.4 us)
Sparse Core Ops, SparseCore 0:
  338.7 89.5 all-gather.2
